TPU v7x, 32 devices: a whole 2x2x4 slice. The times are simulated.
32 devices in a mesh: row: 8 (over z, y), col: 4 (over x, core).
Axes of the slice: x: 2, y: 2, z: 4, core: 2. Of those that a mesh axis runs over, the one named last changes fastest.
Arguments:
- amps: bfloat16 [1024, 4096], P('col', 'row'), may hold values from -6 to 6, as said below
- ints: bfloat16 [2048, 8192], P('col', 'row'), may hold values from -0.125 to 0.125
- block_list: int32 [4, 4], replicated, may hold values from 0 to 1, as said below
Outputs:
- residual: float32 [32, 256, 1024], P(('row', 'col'))
Inputs may be any that keep to these rules, and one draw needn't show every extreme that they name: amps blocks (c, r) and (c, r2) are equal whenever r and r2 agree mod 4. block_list[c, k] is 1 exactly when occupied block c and cd block k carry the same irrep; each block carries one of min(8, 2) irreps, every irrep equally often among occupied blocks and among cd blocks.
All inputs are finite; a program needn't handle non-finite values.
Results may differ from a plain program's by a relative error of at most 0.0003.
Values may be sent and summed in bfloat16 or wider, within the bound.
No kernel may reach another device: no remote copies, remote signals or barrier semaphores. Data moves between devices by JAX's collectives and lax.ppermute only.
A program may use at most 64 MiB of HBM per device.

v0:
```python
import jax
import jax.numpy as jnp
from jax import lax
from jax.sharding import PartitionSpec as P


def shifted(block, axis, distance):
    devices = range(lax.axis_size(axis))
    route = [((i - distance) % len(devices), i) for i in devices]
    return lax.ppermute(block, axis, route)


def shards(amps, ints, block_list):
    row_pos = lax.axis_index("row")
    col_pos = lax.axis_index("col")
    col_count = lax.axis_size("col")
    running = jnp.zeros((amps.shape[0], ints.shape[1]), jnp.float32)
    held_amps = amps
    held_ints = ints
    for offset in range(col_count):
        block_id = (row_pos + col_pos - offset) % col_count
        factor = block_list[col_pos, block_id].astype(jnp.float32)
        running = running + factor * jnp.dot(
            held_amps, held_ints, preferred_element_type=jnp.float32
        )
        if offset + 1 < col_count:
            held_amps = shifted(held_amps, "row", 1)
            held_ints = shifted(held_ints, "col", 1)
    owned = lax.all_to_all(running, "col", split_axis=1, concat_axis=1, tiled=True)
    return owned.reshape(1, owned.shape[0], owned.shape[1])


def solution(mesh):
    placed = (P("col", "row"), P("col", "row"), P())
    return jax.shard_map(
        shards, mesh=mesh, in_specs=placed, out_specs=P(("row", "col"), None, None), check_vma=False
    )
```

profile of v0, /device:TPU:0, one launch (start us, length us, event | category | flops | bytes accessed | tf_op | source)
XLA Modules:
  0.0 75.8 jit_solution(10635011079526394941)
XLA Ops:
  0.0 0.5 collective-permute-start.1
  0.5 14.6 %collective-permute-done.1 = bf16[512,1024]{1,0:T(8,128)(2,1)S(1)} collective-permute-done((bf16[512,1024]{1,0:T(8,128)(2,1)}, bf16[512,1024]{1,0:T(8,128)(2,1)S(1)}, u32[]{:S(2)}, u32[]{:S(2)}) %collective-permute-start.1) | collective-permute-done | bytes 1048608 | tf_op jit(solution)/shard_map/ppermute | solution.py:10
  15.1 0.0 collective-permute-start.3
  15.1 2.3 %collective-permute-start = (bf16[256,512]{1,0:T(8,128)(2,1)}, bf16[256,512]{1,0:T(8,128)(2,1)S(1)}, u32[]{:S(2)}, u32[]{:S(2)}) collective-permute-start(bf16[256,512]{1,0:T(8,128)(2,1)} %param.3), channel_id=1, source_target_pairs={{28,0},{0,4},{4,8},{8,12},{12,16},{16,20},{20,24},{24,28},{29,1},{... | collective-permute-start | bytes 786440 | tf_op jit(solution)/shard_map/ppermute | solution.py:10
  17.4 11.9 %collective-permute-done.3 = bf16[512,1024]{1,0:T(8,128)(2,1)S(1)} collective-permute-done((bf16[512,1024]{1,0:T(8,128)(2,1)S(1)}, bf16[512,1024]{1,0:T(8,128)(2,1)S(1)}, u32[]{:S(2)}, u32[]{:S(2)}) %collective-permute-start.3) | collective-permute-done | bytes 1048608 | tf_op jit(solution)/shard_map/ppermute | solution.py:10
  29.3 0.0 collective-permute-start.5
  29.3 0.0 copy-start
  29.3 0.7 copy-done
  30.0 0.7 fusion.3
  33.2 0.0 collective-permute-done
  33.2 2.4 %collective-permute-start.2 = (bf16[256,512]{1,0:T(8,128)(2,1)S(1)}, bf16[256,512]{1,0:T(8,128)(2,1)S(1)}, u32[]{:S(2)}, u32[]{:S(2)}) collective-permute-start(bf16[256,512]{1,0:T(8,128)(2,1)S(1)} %collective-permute-done), channel_id=1, source_target_pairs={{28,0},{0,4},{4,8},{8,12},{12,16},{16,20},{20,24},{24,28},{29,1},{... | collective-permute-start | bytes 786440 | tf_op jit(solution)/shard_map/ppermute | solution.py:10
  35.6 1.8 %convolution_multiply_fusion.3 = f32[256,1024]{1,0:T(8,128)S(1)} fusion(bf16[256,512]{1,0:T(8,128)(2,1)} %param.3, bf16[512,1024]{1,0:T(8,128)(2,1)} %param.4, f32[]{:T(128)} %bitcast), kind=kOutput, calls=%fused_computation.6 | convolution fusion | flops 268697600 | bytes 2359300 | tf_op jit(solution)/shard_map/dot_general | solution.py:23
  37.4 7.5 %collective-permute-done.2 = bf16[256,512]{1,0:T(8,128)(2,1)S(1)} collective-permute-done((bf16[256,512]{1,0:T(8,128)(2,1)S(1)}, bf16[256,512]{1,0:T(8,128)(2,1)S(1)}, u32[]{:S(2)}, u32[]{:S(2)}) %collective-permute-start.2) | collective-permute-done | bytes 262176 | tf_op jit(solution)/shard_map/ppermute | solution.py:10
  44.9 0.0 collective-permute-start.4
  44.9 0.4 fusion.2
  45.4 0.4 fusion.1
  45.8 10.7 %collective-permute-done.4 = bf16[256,512]{1,0:T(8,128)(2,1)S(1)} collective-permute-done((bf16[256,512]{1,0:T(8,128)(2,1)S(1)}, bf16[256,512]{1,0:T(8,128)(2,1)S(1)}, u32[]{:S(2)}, u32[]{:S(2)}) %collective-permute-start.4) | collective-permute-done | bytes 262176 | tf_op jit(solution)/shard_map/ppermute | solution.py:10
  56.6 0.0 collective-permute-done.5
  56.6 0.4 fusion
  57.0 0.1 copy.10
  57.1 17.1 %all_to_all.9 = f32[256,4,256]{2,0,1:T(8,128)S(1)} all-to-all(f32[256,4,256]{2,0,1:T(8,128)S(1)} %bitcast.18), channel_id=1, replica_groups=mesh['row'=8,'col'=4] {'col'}, dimensions={1} | all-to-all | bytes 2097152 | tf_op jit(solution)/shard_map/all_to_all | solution.py:29
  74.2 0.3 copy.6
  74.5 1.3 %copy.7 = f32[1,256,1024]{2,1,0:T(8,128)} copy(f32[1,256,1024]{1,2,0:T(8,128)S(1)} %bitcast.19) | data formatting | bytes 2097152 | tf_op jit(solution)/shard_map/reshape | solution.py:30
Async XLA Ops:
  0.0 15.1 %collective-permute-start.1 = (bf16[512,1024]{1,0:T(8,128)(2,1)}, bf16[512,1024]{1,0:T(8,128)(2,1)S(1)}, u32[]{:S(2)}, u32[]{:S(2)}) collective-permute-start(bf16[512,1024]{1,0:T(8,128)(2,1)} %param.4), channel_id=1, source_target_pairs={{3,0},{0,1},{1,2},{2,3},{7,4},{4,5},{5,6},{6,7},{11,8},{8,9},{9,10... | collective-permute-start | bytes 3145736 | tf_op jit(solution)/shard_map/ppermute | solution.py:10
  15.1 14.2 %collective-permute-start.3 = (bf16[512,1024]{1,0:T(8,128)(2,1)S(1)}, bf16[512,1024]{1,0:T(8,128)(2,1)S(1)}, u32[]{:S(2)}, u32[]{:S(2)}) collective-permute-start(bf16[512,1024]{1,0:T(8,128)(2,1)S(1)} %collective-permute-done.1), channel_id=1, source_target_pairs={{3,0},{0,1},{1,2},{2,3},{7,4},{4,5},{5,6},{6,7},{11,8},{8,9},{9,10... | collective-permute-start | bytes 3145736 | tf_op jit(solution)/shard_map/ppermute | solution.py:10
  15.1 18.1 %collective-permute-start = (bf16[256,512]{1,0:T(8,128)(2,1)}, bf16[256,512]{1,0:T(8,128)(2,1)S(1)}, u32[]{:S(2)}, u32[]{:S(2)}) collective-permute-start(bf16[256,512]{1,0:T(8,128)(2,1)} %param.3), channel_id=1, source_target_pairs={{28,0},{0,4},{4,8},{8,12},{12,16},{16,20},{20,24},{24,28},{29,1},{... | collective-permute-start | bytes 786440 | tf_op jit(solution)/shard_map/ppermute | solution.py:10
  29.3 27.3 %collective-permute-start.5 = (bf16[512,1024]{1,0:T(8,128)(2,1)S(1)}, bf16[512,1024]{1,0:T(8,128)(2,1)S(1)}, u32[]{:S(2)}, u32[]{:S(2)}) collective-permute-start(bf16[512,1024]{1,0:T(8,128)(2,1)S(1)} %collective-permute-done.3), channel_id=1, source_target_pairs={{3,0},{0,1},{1,2},{2,3},{7,4},{4,5},{5,6},{6,7},{11,8},{8,9},{9,10... | collective-permute-start | bytes 3145736 | tf_op jit(solution)/shard_map/ppermute | solution.py:10
  29.3 0.7 copy-start
  33.2 11.7 %collective-permute-start.2 = (bf16[256,512]{1,0:T(8,128)(2,1)S(1)}, bf16[256,512]{1,0:T(8,128)(2,1)S(1)}, u32[]{:S(2)}, u32[]{:S(2)}) collective-permute-start(bf16[256,512]{1,0:T(8,128)(2,1)S(1)} %collective-permute-done), channel_id=1, source_target_pairs={{28,0},{0,4},{4,8},{8,12},{12,16},{16,20},{20,24},{24,28},{29,1},{... | collective-permute-start | bytes 786440 | tf_op jit(solution)/shard_map/ppermute | solution.py:10
  44.9 11.6 %collective-permute-start.4 = (bf16[256,512]{1,0:T(8,128)(2,1)S(1)}, bf16[256,512]{1,0:T(8,128)(2,1)S(1)}, u32[]{:S(2)}, u32[]{:S(2)}) collective-permute-start(bf16[256,512]{1,0:T(8,128)(2,1)S(1)} %collective-permute-done.2), channel_id=1, source_target_pairs={{28,0},{0,4},{4,8},{8,12},{12,16},{16,20},{20,24},{24,28},{29,1},{... | collective-permute-start | bytes 786440 | tf_op jit(solution)/shard_map/ppermute | solution.py:10
where the time goes:
time: 76.1 us; the launch traced here: 75.8 us
  waiting for transfers between devices  44.8 us (59%)
  blocking collectives  17.1 us (22%)
  starting transfers between devices  5.18 us (7%)
  matrix products  3.08 us (4%)
  local copies, waits for them, and re-layouts  3.07 us (4%)
  between operations  2.66 us (3%)
    ppermute x6, waiting for transfers between devices, shifted(): return lax.ppermute(block, axis, route)  44.8 us
    all_to_all x1, blocking collectives, shards(): lax.all_to_all(running, 'col', split_axis=1, concat_axis=1, tiled=True)  17.1 us
    ppermute x6, starting transfers between devices, shifted(): return lax.ppermute(block, axis, route)  5.18 us
    dot_general x4, matrix products, shards(): jnp.dot(held_amps, held_ints, preferred_element_type=jnp.float32)  3.08 us
  transfers between devices with their start and end apart: 6, of which 4 were waited for; matrix products, arithmetic and copies ran while one was open for 4% of the time, Pallas kernels for 0%

commit v1 on v0

--- a/solution.py
+++ b/solution.py
@@ -26,7 +26,19 @@
         if offset + 1 < col_count:
             held_amps = shifted(held_amps, "row", 1)
             held_ints = shifted(held_ints, "col", 1)
-    owned = lax.all_to_all(running, "col", split_axis=1, concat_axis=1, tiled=True)
+    ways, here = (lax.axis_size("col"), lax.axis_index("col"))
+    width = running.shape[1] // ways
+    shape = list(running.shape)
+    shape[1] = width
+    height = shape[1]
+    shape[1] = height * ways
+    full = jnp.zeros(shape, running.dtype)
+    for mask in range(ways):
+        part = lax.dynamic_slice_in_dim(running, (here ^ mask) * width, width, axis=1)
+        if mask:
+            part = lax.ppermute(part, "col", [(d, d ^ mask) for d in range(ways)])
+        full = lax.dynamic_update_slice_in_dim(full, part, (here ^ mask) * height, axis=1)
+    owned = full
     return owned.reshape(1, owned.shape[0], owned.shape[1])
 
 

time: 76.1 us -> 71.8 us (0.943)
  blocking collectives: 17.1 us -> 0 us
  waiting for transfers between devices: 44.8 us -> 56.6 us
  starting transfers between devices: 5.18 us -> 7.11 us
    all_to_all x1 -> x0, blocking collectives: 17.1 us -> none  [shards(): lax.all_to_all(running, 'col', split_axis=1, concat_axis=1, tiled=True)]
    ppermute x0 -> x3, waiting for transfers between devices: none -> 11.8 us  [shards(): part = lax.ppermute(part, 'col', [(d, d ^ mask) for d in range(ways)])]
    ppermute x0 -> x3, starting transfers between devices: none -> 1.93 us  [shards(): part = lax.ppermute(part, 'col', [(d, d ^ mask) for d in range(ways)])]
    reshape x1, local copies, waits for them, and re-layouts: 1.31 us -> 0.11 us  [shards(): return owned.reshape(1, owned.shape[0], owned.shape[1])]
    dynamic_update_slice x0 -> x4, local copies, waits for them, and re-layouts: none -> 0.8 us  [shards(): lax.dynamic_update_slice_in_dim(full, part, (here ^ mask) * height, axis=1)]
  transfers between devices with their start and end apart: 6 -> 9, of which waited for: 4 -> 6; matrix products, arithmetic and copies ran while one was open for 4% -> 5% of each run, Pallas kernels for 0% -> 0%
where the time goes in v1:
time: 71.8 us; the launch traced here: 71.7 us
  waiting for transfers between devices  56.6 us (79%)
  starting transfers between devices  7.11 us (10%)
  matrix products  3.08 us (4%)
  between operations  2.59 us (4%)
  local copies, waits for them, and re-layouts  2.32 us (3%)
    ppermute x6, waiting for transfers between devices, shifted(): return lax.ppermute(block, axis, route)  44.8 us
    ppermute x3, waiting for transfers between devices, shards(): part = lax.ppermute(part, 'col', [(d, d ^ mask) for d in range(ways)])  11.8 us
    ppermute x6, starting transfers between devices, shifted(): return lax.ppermute(block, axis, route)  5.18 us
    dot_general x4, matrix products, shards(): jnp.dot(held_amps, held_ints, preferred_element_type=jnp.float32)  3.08 us
    ppermute x3, starting transfers between devices, shards(): part = lax.ppermute(part, 'col', [(d, d ^ mask) for d in range(ways)])  1.93 us
  transfers between devices with their start and end apart: 9, of which 6 were waited for; matrix products, arithmetic and copies ran while one was open for 5% of the time, Pallas kernels for 0%

profile of v1, /device:TPU:0, one launch (start us, length us, event | category | flops | bytes accessed | tf_op | source)
XLA Modules:
  0.0 71.7 jit_solution(3235659751015522897)
XLA Ops:
  0.0 0.5 collective-permute-start.1
  0.5 14.6 %collective-permute-done.1 = bf16[512,1024]{1,0:T(8,128)(2,1)S(1)} collective-permute-done((bf16[512,1024]{1,0:T(8,128)(2,1)}, bf16[512,1024]{1,0:T(8,128)(2,1)S(1)}, u32[]{:S(2)}, u32[]{:S(2)}) %collective-permute-start.1) | collective-permute-done | bytes 1048608 | tf_op jit(solution)/shard_map/ppermute | solution.py:10
  15.1 0.0 collective-permute-start.3
  15.1 2.3 %collective-permute-start = (bf16[256,512]{1,0:T(8,128)(2,1)}, bf16[256,512]{1,0:T(8,128)(2,1)S(1)}, u32[]{:S(2)}, u32[]{:S(2)}) collective-permute-start(bf16[256,512]{1,0:T(8,128)(2,1)} %param.3), channel_id=1, source_target_pairs={{28,0},{0,4},{4,8},{8,12},{12,16},{16,20},{20,24},{24,28},{29,1},{... | collective-permute-start | bytes 786440 | tf_op jit(solution)/shard_map/ppermute | solution.py:10
  17.4 11.9 %collective-permute-done.3 = bf16[512,1024]{1,0:T(8,128)(2,1)S(1)} collective-permute-done((bf16[512,1024]{1,0:T(8,128)(2,1)S(1)}, bf16[512,1024]{1,0:T(8,128)(2,1)S(1)}, u32[]{:S(2)}, u32[]{:S(2)}) %collective-permute-start.3) | collective-permute-done | bytes 1048608 | tf_op jit(solution)/shard_map/ppermute | solution.py:10
  29.3 0.0 collective-permute-start.5
  29.3 0.0 copy-start.1
  29.3 0.7 copy-done.1
  30.0 0.6 fusion.3
  33.1 0.0 collective-permute-done
  33.1 2.4 %collective-permute-start.2 = (bf16[256,512]{1,0:T(8,128)(2,1)S(1)}, bf16[256,512]{1,0:T(8,128)(2,1)S(1)}, u32[]{:S(2)}, u32[]{:S(2)}) collective-permute-start(bf16[256,512]{1,0:T(8,128)(2,1)S(1)} %collective-permute-done), channel_id=1, source_target_pairs={{28,0},{0,4},{4,8},{8,12},{12,16},{16,20},{20,24},{24,28},{29,1},{... | collective-permute-start | bytes 786440 | tf_op jit(solution)/shard_map/ppermute | solution.py:10
  35.5 1.8 %convolution_multiply_fusion.3 = f32[256,1024]{1,0:T(8,128)S(1)} fusion(bf16[256,512]{1,0:T(8,128)(2,1)} %param.3, bf16[512,1024]{1,0:T(8,128)(2,1)} %param.4, f32[]{:T(128)} %bitcast), kind=kOutput, calls=%fused_computation.6 | convolution fusion | flops 268697600 | bytes 2359300 | tf_op jit(solution)/shard_map/dot_general | solution.py:23
  37.3 7.5 %collective-permute-done.2 = bf16[256,512]{1,0:T(8,128)(2,1)S(1)} collective-permute-done((bf16[256,512]{1,0:T(8,128)(2,1)S(1)}, bf16[256,512]{1,0:T(8,128)(2,1)S(1)}, u32[]{:S(2)}, u32[]{:S(2)}) %collective-permute-start.2) | collective-permute-done | bytes 262176 | tf_op jit(solution)/shard_map/ppermute | solution.py:10
  44.8 0.0 collective-permute-start.4
  44.8 0.4 fusion.2
  45.3 0.4 fusion.1
  45.7 10.7 %collective-permute-done.4 = bf16[256,512]{1,0:T(8,128)(2,1)S(1)} collective-permute-done((bf16[256,512]{1,0:T(8,128)(2,1)S(1)}, bf16[256,512]{1,0:T(8,128)(2,1)S(1)}, u32[]{:S(2)}, u32[]{:S(2)}) %collective-permute-start.4) | collective-permute-done | bytes 262176 | tf_op jit(solution)/shard_map/ppermute | solution.py:10
  56.4 0.0 collective-permute-done.5
  56.4 0.4 fusion
  56.9 0.1 constant_dynamic-slice_fusion
  57.0 0.1 collective-permute-start.6
  57.0 1.6 %collective-permute-start.7 = (f32[256,256]{1,0:T(8,128)S(1)}, f32[256,256]{1,0:T(8,128)S(1)}, u32[]{:S(2)}, u32[]{:S(2)}) collective-permute-start(f32[256,256]{1,0:T(8,128)S(1)} %get-tuple-element.6), channel_id=1, source_target_pairs={{0,2},{1,3},{2,0},{3,1},{4,6},{5,7},{6,4},{7,5},{8,10},{9,11},{10,... | collective-permute-start | bytes 786440 | tf_op jit(solution)/shard_map/ppermute | solution.py:39
  58.6 0.3 collective-permute-start.8
  58.9 0.1 reshape.23
  59.1 0.0 collective-permute-done.6
  59.1 7.1 %collective-permute-done.7 = f32[256,256]{1,0:T(8,128)S(1)} collective-permute-done((f32[256,256]{1,0:T(8,128)S(1)}, f32[256,256]{1,0:T(8,128)S(1)}, u32[]{:S(2)}, u32[]{:S(2)}) %collective-permute-start.7) | collective-permute-done | bytes 262176 | tf_op jit(solution)/shard_map/ppermute | solution.py:39
  66.3 0.0 copy-start
  66.3 4.7 %collective-permute-done.8 = f32[256,256]{1,0:T(8,128)S(1)} collective-permute-done((f32[256,256]{1,0:T(8,128)S(1)}, f32[256,256]{1,0:T(8,128)S(1)}, u32[]{:S(2)}, u32[]{:S(2)}) %collective-permute-start.8) | collective-permute-done | bytes 262176 | tf_op jit(solution)/shard_map/ppermute | solution.py:39
  70.9 0.0 copy-done
  70.9 0.7 %bitcast_dynamic-update-slice_fusion = f32[1,256,1024]{2,1,0:T(8,128)} fusion(f32[1,256,1024]{2,1,0:T(8,128)} %copy-done, s32[]{:T(128)S(6)} %select_n.65, f32[256,256]{1,0:T(8,128)S(1)} %collective-permute-done.8), kind=kLoop, calls=%fused_computation.7 | loop fusion | bytes 524292 | tf_op jit(solution)/shard_map/dynamic_update_slice | solution.py:40
  (3 shorter events, 0.1 us)
Async XLA Ops:
  0.0 15.1 %collective-permute-start.1 = (bf16[512,1024]{1,0:T(8,128)(2,1)}, bf16[512,1024]{1,0:T(8,128)(2,1)S(1)}, u32[]{:S(2)}, u32[]{:S(2)}) collective-permute-start(bf16[512,1024]{1,0:T(8,128)(2,1)} %param.4), channel_id=1, source_target_pairs={{3,0},{0,1},{1,2},{2,3},{7,4},{4,5},{5,6},{6,7},{11,8},{8,9},{9,10... | collective-permute-start | bytes 3145736 | tf_op jit(solution)/shard_map/ppermute | solution.py:10
  15.1 14.2 %collective-permute-start.3 = (bf16[512,1024]{1,0:T(8,128)(2,1)S(1)}, bf16[512,1024]{1,0:T(8,128)(2,1)S(1)}, u32[]{:S(2)}, u32[]{:S(2)}) collective-permute-start(bf16[512,1024]{1,0:T(8,128)(2,1)S(1)} %collective-permute-done.1), channel_id=1, source_target_pairs={{3,0},{0,1},{1,2},{2,3},{7,4},{4,5},{5,6},{6,7},{11,8},{8,9},{9,10... | collective-permute-start | bytes 3145736 | tf_op jit(solution)/shard_map/ppermute | solution.py:10
  15.1 18.0 %collective-permute-start = (bf16[256,512]{1,0:T(8,128)(2,1)}, bf16[256,512]{1,0:T(8,128)(2,1)S(1)}, u32[]{:S(2)}, u32[]{:S(2)}) collective-permute-start(bf16[256,512]{1,0:T(8,128)(2,1)} %param.3), channel_id=1, source_target_pairs={{28,0},{0,4},{4,8},{8,12},{12,16},{16,20},{20,24},{24,28},{29,1},{... | collective-permute-start | bytes 786440 | tf_op jit(solution)/shard_map/ppermute | solution.py:10
  29.3 27.1 %collective-permute-start.5 = (bf16[512,1024]{1,0:T(8,128)(2,1)S(1)}, bf16[512,1024]{1,0:T(8,128)(2,1)S(1)}, u32[]{:S(2)}, u32[]{:S(2)}) collective-permute-start(bf16[512,1024]{1,0:T(8,128)(2,1)S(1)} %collective-permute-done.3), channel_id=1, source_target_pairs={{3,0},{0,1},{1,2},{2,3},{7,4},{4,5},{5,6},{6,7},{11,8},{8,9},{9,10... | collective-permute-start | bytes 3145736 | tf_op jit(solution)/shard_map/ppermute | solution.py:10
  29.3 0.7 copy-start.1
  33.1 11.7 %collective-permute-start.2 = (bf16[256,512]{1,0:T(8,128)(2,1)S(1)}, bf16[256,512]{1,0:T(8,128)(2,1)S(1)}, u32[]{:S(2)}, u32[]{:S(2)}) collective-permute-start(bf16[256,512]{1,0:T(8,128)(2,1)S(1)} %collective-permute-done), channel_id=1, source_target_pairs={{28,0},{0,4},{4,8},{8,12},{12,16},{16,20},{20,24},{24,28},{29,1},{... | collective-permute-start | bytes 786440 | tf_op jit(solution)/shard_map/ppermute | solution.py:10
  44.8 11.6 %collective-permute-start.4 = (bf16[256,512]{1,0:T(8,128)(2,1)S(1)}, bf16[256,512]{1,0:T(8,128)(2,1)S(1)}, u32[]{:S(2)}, u32[]{:S(2)}) collective-permute-start(bf16[256,512]{1,0:T(8,128)(2,1)S(1)} %collective-permute-done.2), channel_id=1, source_target_pairs={{28,0},{0,4},{4,8},{8,12},{12,16},{16,20},{20,24},{24,28},{29,1},{... | collective-permute-start | bytes 786440 | tf_op jit(solution)/shard_map/ppermute | solution.py:10
  57.0 2.1 %collective-permute-start.6 = (f32[256,256]{1,0:T(8,128)S(1)}, f32[256,256]{1,0:T(8,128)S(1)}, u32[]{:S(2)}, u32[]{:S(2)}) collective-permute-start(f32[256,256]{1,0:T(8,128)S(1)} %get-tuple-element.7), channel_id=1, source_target_pairs={{0,1},{1,0},{2,3},{3,2},{4,5},{5,4},{6,7},{7,6},{8,9},{9,8},{10,11... | collective-permute-start | bytes 786440 | tf_op jit(solution)/shard_map/ppermute | solution.py:39
  57.0 9.2 %collective-permute-start.7 = (f32[256,256]{1,0:T(8,128)S(1)}, f32[256,256]{1,0:T(8,128)S(1)}, u32[]{:S(2)}, u32[]{:S(2)}) collective-permute-start(f32[256,256]{1,0:T(8,128)S(1)} %get-tuple-element.6), channel_id=1, source_target_pairs={{0,2},{1,3},{2,0},{3,1},{4,6},{5,7},{6,4},{7,5},{8,10},{9,11},{10,... | collective-permute-start | bytes 786440 | tf_op jit(solution)/shard_map/ppermute | solution.py:39
  58.6 12.3 %collective-permute-start.8 = (f32[256,256]{1,0:T(8,128)S(1)}, f32[256,256]{1,0:T(8,128)S(1)}, u32[]{:S(2)}, u32[]{:S(2)}) collective-permute-start(f32[256,256]{1,0:T(8,128)S(1)} %get-tuple-element.5), channel_id=1, source_target_pairs={{0,3},{1,2},{2,1},{3,0},{4,7},{5,6},{6,5},{7,4},{8,11},{9,10},{10,... | collective-permute-start | bytes 786440 | tf_op jit(solution)/shard_map/ppermute | solution.py:39
  66.3 4.7 %copy-start = (f32[1,256,1024]{2,1,0:T(8,128)}, f32[1,256,1024]{2,1,0:T(8,128)S(1)}, u32[]{:S(2)}) copy-start(f32[1,256,1024]{2,1,0:T(8,128)S(1)} %bitcast_dynamic-update-slice_fusion.1) | copy-start | bytes 3145732
